TPU v7x, 512 devices: a whole 4x8x8 slice. The times are simulated.
512 devices in a mesh: band: 64 (over y, z), lev: 8 (over x, core).
Axes of the slice: x: 4, y: 8, z: 8, core: 2. Of those that a mesh axis runs over, the one named last changes fastest.
Arguments:
- concentration: float32 [4, 8, 128, 256], P(None, 'lev', 'band'), may hold values from 0.1 to 2
- target: float32 [4, 8, 128, 256], P(None, 'lev', 'band'), may hold values from -6 to 6
- zonal_wind: float32 [8, 128, 256], P('lev', 'band'), may hold values from -0.6 to 0.6
- merid_wind: float32 [8, 128, 256], P('lev', 'band'), may hold values from -0.6 to 0.6
- sea_mask: int32 [128, 256], P('band'), may hold values 0 or 1
- first_weight: float32 [2, 20, 128], replicated, may hold values from -1.25 to 1.25
- first_bias: float32 [2, 128], replicated, may hold values from -3 to 3
- middle_weight: float32 [2, 128, 128], replicated, may hold values from -0.5 to 0.5
- middle_bias: float32 [2, 128], replicated, may hold values from -3 to 3
- last_weight: float32 [2, 4, 128], replicated, may hold values from -0.125 to 0.125
- last_bias: float32 [2, 4], replicated, may hold values from -0.6 to 0.6
Outputs:
- final_field: float32 [4, 8, 128, 256], P(None, 'lev', 'band')
- first_weight_grad: float32 [2, 20, 128], replicated
- first_bias_grad: float32 [2, 128], replicated
- middle_weight_grad: float32 [2, 128, 128], replicated
- middle_bias_grad: float32 [2, 128], replicated
- last_weight_grad: float32 [2, 4, 128], replicated
- last_bias_grad: float32 [2, 4], replicated
Inputs may be any that keep to these rules, and one draw needn't show every extreme that they name: `sea_mask`: 1 marks a sea cell, 0 a land cell.
All inputs are finite; a program needn't handle non-finite values. No bound on the sum of `sea_mask` on one device may be relied on, other than what follows from the above.
Results may differ from a plain program's by a relative error of at most 0.00013.
Values sent between devices are 32-bit elements; how exact they have to be, the bound alone decides.
A program may use at most 64 MiB of HBM per device.

v0:
```python
import math
import jax
import jax.numpy as jnp
from jax import lax
from jax.sharding import PartitionSpec as P

STEPS = 3
stencil_base = (-1.0 / 12.0, 7.0 / 12.0, 7.0 / 12.0, -1.0 / 12.0)


def cut_along(array, direction, start, length):
    return lax.slice_in_dim(array, start, start + length, axis=direction)


def pad_along(array, direction, width):
    widths = [(0, 0)] * array.ndim
    widths[direction] = (width, width)
    return jnp.pad(array, widths)


def face_flux(network, stencil, courant, mask_low, mask_high):
    w_first, b_first, w_second, b_second, w_last, b_last = network
    face_shape = courant.shape
    columns = courant.size
    nbins = stencil.shape[1]
    features = jnp.concatenate(
        [
            stencil.reshape(4 * nbins, columns),
            courant.reshape(1, columns),
            (courant * courant).reshape(1, columns),
            mask_low.reshape(1, columns),
            mask_high.reshape(1, columns),
        ],
        0,
    )
    hidden_one = jnp.tanh(
        jnp.dot(w_first.T, features, precision=lax.Precision.HIGHEST) + b_first[:, None]
    )
    hidden_two = jnp.tanh(
        jnp.dot(w_second.T, hidden_one, precision=lax.Precision.HIGHEST) + b_second[:, None]
    )
    output = jnp.dot(w_last, hidden_two, precision=lax.Precision.HIGHEST) + b_last[:, None]
    correction = output - jnp.mean(output, 0, keepdims=True)
    weights_face = jnp.asarray(stencil_base, jnp.float32)[:, None] + correction
    face_value = jnp.sum(weights_face.reshape((4, 1) + face_shape) * stencil, 0)
    return courant[None] * face_value


def advance(network, padded, wind_padded, mask_padded, direction):
    length = padded.shape[direction] - 4
    stencil = jnp.stack([cut_along(padded, direction, offset, length + 1) for offset in range(4)])
    courant = 0.5 * (
        cut_along(wind_padded, direction - 1, 0, length + 1)
        + cut_along(wind_padded, direction - 1, 1, length + 1)
    )
    mask_low = cut_along(mask_padded, direction - 1, 0, length + 1)
    mask_high = cut_along(mask_padded, direction - 1, 1, length + 1)
    fluxes = face_flux(network, stencil, courant, mask_low, mask_high)
    centre = cut_along(padded, direction, 2, length)
    return centre - (
        cut_along(fluxes, direction, 1, length) - cut_along(fluxes, direction, 0, length)
    )


def to_columns(field):
    return lax.all_to_all(field, "band", split_axis=3, concat_axis=2, tiled=True)


def to_rows(field):
    return lax.all_to_all(field, "band", split_axis=2, concat_axis=3, tiled=True)


def on_device(
    concentration,
    target,
    zonal_wind,
    merid_wind,
    sea_mask,
    first_weight,
    first_bias,
    middle_weight,
    middle_bias,
    last_weight,
    last_bias,
):
    params = (first_weight, first_bias, middle_weight, middle_bias, last_weight, last_bias)
    zonal_net = tuple((member[0] for member in params))
    merid_net = tuple((member[1] for member in params))
    bins_here, levels_here, row_count, col_count = concentration.shape
    total_cells = (
        bins_here
        * levels_here
        * row_count
        * col_count
        * lax.axis_size("band")
        * lax.axis_size("lev")
    )
    loss_scale = 1.0 / math.sqrt(total_cells)
    sea_field = sea_mask.astype(jnp.float32)[None]
    wind_zonal = pad_along(zonal_wind, 2, 1)
    mask_zonal = pad_along(sea_field, 2, 1)
    stacked = jnp.concatenate([merid_wind, sea_field], 0)
    columns_data = lax.all_to_all(stacked, "band", split_axis=2, concat_axis=1, tiled=True)
    wind_merid = pad_along(columns_data[:levels_here], 1, 1)
    mask_merid = pad_along(columns_data[levels_here:], 1, 1)

    def zonal_sweep(network, padded):
        return advance(network, padded, wind_zonal, mask_zonal, 3)

    def merid_sweep(network, padded):
        return advance(network, padded, wind_merid, mask_merid, 2)

    pullbacks = []
    field = concentration
    for step_number in range(STEPS):
        field, zonal_back = jax.vjp(zonal_sweep, zonal_net, pad_along(field, 3, 2))
        moved, merid_back = jax.vjp(merid_sweep, merid_net, pad_along(to_columns(field), 2, 2))
        field = to_rows(moved)
        pullbacks.append((zonal_back, merid_back))
    cotangent = (field - target) * loss_scale
    sums = tuple((jnp.zeros_like(member) for member in params))
    for step_number in reversed(range(STEPS)):
        zonal_back, merid_back = pullbacks[step_number]
        merid_grads, padded_grad = merid_back(to_columns(cotangent))
        cotangent = to_rows(padded_grad[:, :, 2:-2])
        zonal_grads, padded_grad = zonal_back(cotangent)
        cotangent = padded_grad[:, :, :, 2:-2]
        step_grads = tuple(
            (
                jnp.stack([zonal_part, merid_part])
                for zonal_part, merid_part in zip(zonal_grads, merid_grads)
            )
        )
        sums = tuple((earlier + latest for earlier, latest in zip(sums, step_grads)))
    sums = lax.psum((sums[0], sums[1], sums[2], sums[3], sums[4], sums[5]), ("band", "lev"))
    return (field, sums[0], sums[1], sums[2], sums[3], sums[4], sums[5])


def solution(mesh):
    return jax.shard_map(
        on_device,
        mesh=mesh,
        in_specs=(
            P(None, "lev", "band", None),
            P(None, "lev", "band", None),
            P("lev", "band", None),
            P("lev", "band", None),
            P("band", None),
            P(),
            P(),
            P(),
            P(),
            P(),
            P(),
        ),
        out_specs=(P(None, "lev", "band", None), P(), P(), P(), P(), P(), P()),
        check_vma=False,
    )
```

profile of v0, /device:TPU:1, one launch (start us, length us, event | category | flops | bytes accessed | tf_op | source)
XLA Modules:
  0.0 649.2 jit_solution(2578516520645093349)
XLA Ops:
  9.5 17.3 %all-to-all-start.1 = ((f32[2,2,256]{1,0,2:T(2,128)}), f32[2,2,256]{1,0,2:T(2,128)S(1)}, u32[]{:S(2)}, u32[]{:S(2)}) async-start(f32[2,2,256]{1,0,2:T(2,128)} %copy.634), calls=%async_computation.1 | async-start | bytes 524288 | tf_op jit(solution)/shard_map/all_to_all | solution.py:103
  36.5 3.0 all-to-all-done.1
  39.6 9.1 %all-to-all-start = ((f32[4,1,2,256]{0,2,1,3:T(2,128)}), f32[4,1,2,256]{0,2,1,3:T(2,128)S(1)}, u32[]{:S(2)}, u32[]{:S(2)}) async-start(f32[4,1,2,256]{0,2,1,3:T(2,128)} %copy.631), calls=%async_computation | async-start | bytes 524288 | tf_op jit(solution)/shard_map/all_to_all | solution.py:66
  50.4 10.8 %all-to-all-done = f32[4,1,2,256]{0,2,1,3:T(2,128)S(1)} async-done(((f32[4,1,2,256]{0,2,1,3:T(2,128)}), f32[4,1,2,256]{0,2,1,3:T(2,128)S(1)}, u32[]{:S(2)}, u32[]{:S(2)}) %all-to-all-start) | async-done | bytes 8224 | tf_op jit(solution)/shard_map/all_to_all | solution.py:66
  66.5 18.4 %all_to_all.231 = f32[4,1,128,4]{3,0,1,2:T(4,128)S(1)} all-to-all(f32[4,1,128,4]{3,0,1,2:T(4,128)S(1)} %copy.642), channel_id=1, replica_groups=mesh['band'=64,'lev'=8] {'band'}, dimensions={2} | all-to-all | bytes 16384 | tf_op jit(solution)/shard_map/all_to_all | solution.py:70
  88.9 18.4 %all_to_all.232 = f32[4,1,2,256]{0,2,1,3:T(2,128)S(1)} all-to-all(f32[4,1,2,256]{0,2,1,3:T(2,128)S(1)} %copy.646), channel_id=1, replica_groups=mesh['band'=64,'lev'=8] {'band'}, dimensions={3} | all-to-all | bytes 16384 | tf_op jit(solution)/shard_map/all_to_all | solution.py:66
  117.3 18.4 %all_to_all.233 = f32[4,1,128,4]{3,0,1,2:T(4,128)S(1)} all-to-all(f32[4,1,128,4]{3,0,1,2:T(4,128)S(1)} %copy.651), channel_id=1, replica_groups=mesh['band'=64,'lev'=8] {'band'}, dimensions={2} | all-to-all | bytes 16384 | tf_op jit(solution)/shard_map/all_to_all | solution.py:70
  139.6 18.4 %all_to_all.234 = f32[4,1,2,256]{0,2,1,3:T(2,128)S(1)} all-to-all(f32[4,1,2,256]{0,2,1,3:T(2,128)S(1)} %copy.655), channel_id=1, replica_groups=mesh['band'=64,'lev'=8] {'band'}, dimensions={3} | all-to-all | bytes 16384 | tf_op jit(solution)/shard_map/all_to_all | solution.py:66
  163.3 2.2 reshape.1580
  165.5 2.7 concatenate.123
  175.5 1.9 multiply_reduce_fusion
  177.4 1.7 copy.716
  182.8 18.8 %all_to_all.235 = f32[4,1,128,4]{3,0,1,2:T(4,128)S(1)} all-to-all(f32[4,1,128,4]{3,0,1,2:T(4,128)} %copy.660), channel_id=1, replica_groups=mesh['band'=64,'lev'=8] {'band'}, dimensions={2} | all-to-all | bytes 16384 | tf_op jit(solution)/shard_map/all_to_all | solution.py:70
  202.4 1.7 all_to_all.193
  207.0 18.1 %all_to_all.236 = f32[4,1,2,256]{0,2,1,3:T(2,128)} all-to-all(f32[4,1,2,256]{0,2,1,3:T(2,128)} %copy.664), channel_id=1, replica_groups=mesh['band'=64,'lev'=8] {'band'}, dimensions={3} | all-to-all | bytes 16384 | tf_op jit(solution)/shard_map/all_to_all | solution.py:66
  225.2 2.6 copy.711
  227.8 1.9 copy.666
  229.7 1.7 copy.667
  235.0 1.9 multiply_reduce_fusion.7
  237.6 1.7 reshape.1587
  250.9 4.7 all-to-all-start.8
  257.2 11.0 %all-to-all-done.8 = f32[4,1,128,4]{3,0,1,2:T(4,128)S(1)} async-done(((f32[4,1,128,4]{3,0,1,2:T(4,128)}), f32[4,1,128,4]{3,0,1,2:T(4,128)S(1)}, u32[]{:S(2)}, u32[]{:S(2)}) %all-to-all-start.8) | async-done | bytes 8224 | tf_op jit(solution)/shard_map/all_to_all | solution.py:70
  275.7 5.0 all-to-all-start.9
  281.5 11.8 %all-to-all-done.9 = f32[4,1,2,256]{0,2,1,3:T(2,128)S(1)} async-done(((f32[4,1,2,256]{0,2,1,3:T(2,128)}), f32[4,1,2,256]{0,2,1,3:T(2,128)S(1)}, u32[]{:S(2)}, u32[]{:S(2)}) %all-to-all-start.9) | async-done | bytes 8224 | tf_op jit(solution)/shard_map/all_to_all | solution.py:66
  305.4 4.7 all-to-all-start.10
  310.4 12.3 %all-to-all-done.10 = f32[4,1,128,4]{3,0,1,2:T(4,128)S(1)} async-done(((f32[4,1,128,4]{3,0,1,2:T(4,128)}), f32[4,1,128,4]{3,0,1,2:T(4,128)S(1)}, u32[]{:S(2)}, u32[]{:S(2)}) %all-to-all-start.10) | async-done | bytes 8224 | tf_op jit(solution)/shard_map/all_to_all | solution.py:70
  327.3 4.8 all-to-all-start.11
  332.3 12.3 %all-to-all-done.11 = f32[4,1,2,256]{0,2,1,3:T(2,128)S(1)} async-done(((f32[4,1,2,256]{0,2,1,3:T(2,128)}), f32[4,1,2,256]{0,2,1,3:T(2,128)S(1)}, u32[]{:S(2)}, u32[]{:S(2)}) %all-to-all-start.11) | async-done | bytes 8224 | tf_op jit(solution)/shard_map/all_to_all | solution.py:66
  351.7 4.7 all-to-all-start.12
  356.7 12.2 %all-to-all-done.12 = f32[4,1,128,4]{3,0,1,2:T(4,128)S(1)} async-done(((f32[4,1,128,4]{3,0,1,2:T(4,128)}), f32[4,1,128,4]{3,0,1,2:T(4,128)S(1)}, u32[]{:S(2)}, u32[]{:S(2)}) %all-to-all-start.12) | async-done | bytes 8224 | tf_op jit(solution)/shard_map/all_to_all | solution.py:70
  373.4 104.7 %all-reduce.47 = (f32[2,20,128]{2,1,0:T(8,128)S(1)}, f32[2,128]{1,0:T(2,128)}, f32[2,128]{1,0:T(2,128)}, f32[2,4,128]{2,1,0:T(4,128)}, f32[2,4]{1,0:T(2,128)}) all-reduce(f32[2,20,128]{2,1,0:T(8,128)S(1)} %fusion.37, f32[2,128]{1,0:T(2,128)S(1)} %get-tuple-element.216, ...), channel_id=1, replica_groups=mesh['band'=64,'lev'=8] {'band','lev'}, use_global_device_ids=true, to_apply=%region_24.25 | all-reduce | flops 6664 | bytes 53312 | tf_op jit(solution)/shard_map/psum | solution.py:135
  478.7 161.8 %all-reduce.50.cloned.1.call-done = f32[2,128,128]{2,1,0:T(8,128)} async-done(((f32[2,128,128]{2,1,0:T(8,128)}), f32[2,128,128]{2,1,0:T(8,128)}) %all-reduce.50.cloned.1.call-update) | async-done | bytes 131088 | tf_op jit(solution)/shard_map/psum | solution.py:135
  (509 shorter events, 111.7 us)
Async XLA Ops:
  7.2 26.5 %copy-start = (f32[2,128,128]{2,1,0:T(8,128)S(1)}, f32[2,128,128]{2,1,0:T(8,128)}, u32[]{:S(2)}) copy-start(f32[2,128,128]{2,1,0:T(8,128)} %param.24) | copy-start | bytes 393220
  8.6 26.4 %copy-start.73 = (f32[2,4,128]{2,1,0:T(4,128)S(1)}, f32[2,4,128]{2,1,0:T(4,128)}, u32[]{:S(2)}) copy-start(f32[2,4,128]{2,1,0:T(4,128)} %param.26) | copy-start | bytes 12292
  9.5 25.9 %copy-start.100 = (f32[4]{0:T(128)S(1)}, f32[4]{0:T(128)}, u32[]{:S(2)}) copy-start(f32[4]{0:T(128)} %constant.29.clone) | copy-start | bytes 52
  9.5 26.1 %copy-start.82 = (f32[4,1,2,256]{3,2,1,0:T(2,128)S(1)}, f32[4,1,2,256]{3,2,1,0:T(2,128)}, u32[]{:S(2)}) copy-start(f32[4,1,2,256]{3,2,1,0:T(2,128)} %param.17) | copy-start | bytes 24580
  9.5 30.1 %all-to-all-start.1 = ((f32[2,2,256]{1,0,2:T(2,128)}), f32[2,2,256]{1,0,2:T(2,128)S(1)}, u32[]{:S(2)}, u32[]{:S(2)}) async-start(f32[2,2,256]{1,0,2:T(2,128)} %copy.634), calls=%async_computation.1 | async-start | bytes 524288 | tf_op jit(solution)/shard_map/all_to_all | solution.py:103
  29.1 34.0 %copy-start.103 = (f32[128]{0:T(128)}, f32[128]{0:T(128)S(1)}, u32[]{:S(2)}) copy-start(f32[128]{0:T(128)S(1)} %get-tuple-element.178) | copy-start | bytes 1540
  29.1 56.4 %copy-start.105 = (f32[128]{0:T(128)}, f32[128]{0:T(128)S(1)}, u32[]{:S(2)}) copy-start(f32[128]{0:T(128)S(1)} %get-tuple-element.179) | copy-start | bytes 1540
  29.9 34.0 %copy-start.111 = (f32[128]{0:T(128)}, f32[128]{0:T(128)S(1)}, u32[]{:S(2)}) copy-start(f32[128]{0:T(128)S(1)} %get-tuple-element.176) | copy-start | bytes 1540
  29.9 56.3 %copy-start.112 = (f32[128]{0:T(128)}, f32[128]{0:T(128)S(1)}, u32[]{:S(2)}) copy-start(f32[128]{0:T(128)S(1)} %get-tuple-element.177) | copy-start | bytes 1540
  30.6 33.8 %copy-start.104 = (f32[4]{0:T(128)}, f32[4]{0:T(128)S(1)}, u32[]{:S(2)}) copy-start(f32[4]{0:T(128)S(1)} %get-tuple-element.174) | copy-start | bytes 52
  30.6 56.1 %copy-start.107 = (f32[4]{0:T(128)}, f32[4]{0:T(128)S(1)}, u32[]{:S(2)}) copy-start(f32[4]{0:T(128)S(1)} %get-tuple-element.175) | copy-start | bytes 52
  30.7 54.7 %copy-start.91 = (f32[1,514]{1,0:T(1,128)}, f32[1,514]{1,0:T(1,128)S(1)}, u32[]{:S(2)}) copy-start(f32[1,514]{1,0:T(1,128)S(1)} %reshape.1571) | copy-start | bytes 6172
  30.8 54.6 %copy-start.93 = (f32[1,514]{1,0:T(1,128)}, f32[1,514]{1,0:T(1,128)S(1)}, u32[]{:S(2)}) copy-start(f32[1,514]{1,0:T(1,128)S(1)} %reshape.1570) | copy-start | bytes 6172
  31.7 53.7 %copy-start.95 = (f32[1,514]{1,0:T(1,128)}, f32[1,514]{1,0:T(1,128)S(1)}, u32[]{:S(2)}) copy-start(f32[1,514]{1,0:T(1,128)S(1)} %reshape.1569) | copy-start | bytes 6172
  31.8 53.6 %copy-start.97 = (f32[1,514]{1,0:T(1,128)}, f32[1,514]{1,0:T(1,128)S(1)}, u32[]{:S(2)}) copy-start(f32[1,514]{1,0:T(1,128)S(1)} %reshape.1568) | copy-start | bytes 6172
  32.7 52.8 %copy-start.43 = (f32[1,20,128]{2,0,1:T(1,128)}, f32[1,20,128]{2,0,1:T(1,128)S(1)}, u32[]{:S(2)}) copy-start(f32[1,20,128]{2,0,1:T(1,128)S(1)} %get-tuple-element.154) | copy-start | bytes 30724
  39.6 21.6 %all-to-all-start = ((f32[4,1,2,256]{0,2,1,3:T(2,128)}), f32[4,1,2,256]{0,2,1,3:T(2,128)S(1)}, u32[]{:S(2)}, u32[]{:S(2)}) async-start(f32[4,1,2,256]{0,2,1,3:T(2,128)} %copy.631), calls=%async_computation | async-start | bytes 524288 | tf_op jit(solution)/shard_map/all_to_all | solution.py:66
  116.6 19.5 %copy-start.92 = (f32[1,514]{1,0:T(1,128)S(1)}, f32[1,514]{1,0:T(1,128)}, u32[]{:S(2)}) copy-start(f32[1,514]{1,0:T(1,128)} %copy-done.91) | copy-start | bytes 6172
  116.6 19.5 %copy-start.94 = (f32[1,514]{1,0:T(1,128)S(1)}, f32[1,514]{1,0:T(1,128)}, u32[]{:S(2)}) copy-start(f32[1,514]{1,0:T(1,128)} %copy-done.93) | copy-start | bytes 6172
  116.7 19.5 %copy-start.96 = (f32[1,514]{1,0:T(1,128)S(1)}, f32[1,514]{1,0:T(1,128)}, u32[]{:S(2)}) copy-start(f32[1,514]{1,0:T(1,128)} %copy-done.95) | copy-start | bytes 6172
  116.7 19.5 %copy-start.44 = (f32[1,20,128]{2,0,1:T(1,128)S(1)}, f32[1,20,128]{2,0,1:T(1,128)}, u32[]{:S(2)}) copy-start(f32[1,20,128]{2,0,1:T(1,128)} %copy-done.43) | copy-start | bytes 30724
  116.7 19.5 %copy-start.106 = (f32[128]{0:T(128)S(1)}, f32[128]{0:T(128)}, u32[]{:S(2)}) copy-start(f32[128]{0:T(128)} %copy-done.105) | copy-start | bytes 1540
  117.1 19.8 %copy-start.113 = (f32[128]{0:T(128)S(1)}, f32[128]{0:T(128)}, u32[]{:S(2)}) copy-start(f32[128]{0:T(128)} %copy-done.112) | copy-start | bytes 1540
  250.0 19.6 %copy-start.10 = (f32[514,128]{1,0:T(8,128)S(1)}, f32[514,128]{1,0:T(8,128)}, u32[]{:S(2)}) copy-start(f32[514,128]{1,0:T(8,128)} %copy-done.9) | copy-start | bytes 789508
  250.0 19.6 %copy-start.76 = (f32[2,4,128]{2,1,0:T(4,128)S(1)}, f32[2,4,128]{2,1,0:T(4,128)}, u32[]{:S(2)}) copy-start(f32[2,4,128]{2,1,0:T(4,128)} %param.26) | copy-start | bytes 12292
  250.9 19.9 %copy-start.23 = (f32[514,128]{1,0:T(8,128)S(1)}, f32[514,128]{1,0:T(8,128)}, u32[]{:S(2)}) copy-start(f32[514,128]{1,0:T(8,128)} %copy-done.22) | copy-start | bytes 789508
  250.9 17.3 %all-to-all-start.8 = ((f32[4,1,128,4]{3,0,1,2:T(4,128)}), f32[4,1,128,4]{3,0,1,2:T(4,128)S(1)}, u32[]{:S(2)}, u32[]{:S(2)}) async-start(f32[4,1,128,4]{3,0,1,2:T(4,128)} %copy.671), calls=%async_computation.8 | async-start | bytes 524288 | tf_op jit(solution)/shard_map/all_to_all | solution.py:70
  275.7 17.6 %all-to-all-start.9 = ((f32[4,1,2,256]{0,2,1,3:T(2,128)}), f32[4,1,2,256]{0,2,1,3:T(2,128)S(1)}, u32[]{:S(2)}, u32[]{:S(2)}) async-start(f32[4,1,2,256]{0,2,1,3:T(2,128)} %copy.677), calls=%async_computation.9 | async-start | bytes 524288 | tf_op jit(solution)/shard_map/all_to_all | solution.py:66
  305.4 17.3 %all-to-all-start.10 = ((f32[4,1,128,4]{3,0,1,2:T(4,128)}), f32[4,1,128,4]{3,0,1,2:T(4,128)S(1)}, u32[]{:S(2)}, u32[]{:S(2)}) async-start(f32[4,1,128,4]{3,0,1,2:T(4,128)} %copy.684), calls=%async_computation.10 | async-start | bytes 524288 | tf_op jit(solution)/shard_map/all_to_all | solution.py:70
  327.3 17.3 %all-to-all-start.11 = ((f32[4,1,2,256]{0,2,1,3:T(2,128)}), f32[4,1,2,256]{0,2,1,3:T(2,128)S(1)}, u32[]{:S(2)}, u32[]{:S(2)}) async-start(f32[4,1,2,256]{0,2,1,3:T(2,128)} %copy.690), calls=%async_computation.11 | async-start | bytes 524288 | tf_op jit(solution)/shard_map/all_to_all | solution.py:66
  351.7 17.3 %all-to-all-start.12 = ((f32[4,1,128,4]{3,0,1,2:T(4,128)}), f32[4,1,128,4]{3,0,1,2:T(4,128)S(1)}, u32[]{:S(2)}, u32[]{:S(2)}) async-start(f32[4,1,128,4]{3,0,1,2:T(4,128)} %copy.697), calls=%async_computation.12 | async-start | bytes 524288 | tf_op jit(solution)/shard_map/all_to_all | solution.py:70
  356.4 284.2 %all-reduce.50.cloned.1.call-start = ((), (), s32[]{:S(2)}) async-start(), calls=%async_computation.13 | async-start | bytes 262144 | tf_op jit(solution)/shard_map/psum | solution.py:135
  (99 other events, 596.4 us)
Sparse Core Ops, SparseCore 0:
  373.0 267.4 all-reduce.49
where the time goes:
time: 660 us; the launch traced here: 649 us
  waiting for transfers between devices  235 us (36%)
  blocking collectives  215 us (33%)
  local copies, waits for them, and re-layouts  70 us (11%)
  starting transfers between devices  50.5 us (8%)
  matrix products  39.1 us (6%)
  other arithmetic  22.5 us (3%)
  between operations  16.6 us (3%)
    psum x1, waiting for transfers between devices, on_device(): lax.psum((sums[0], sums[1], sums[2], sums[3], sums[4], sums[5]), ('band',...  162 us
    psum x1, blocking collectives, on_device(): lax.psum((sums[0], sums[1], sums[2], sums[3], sums[4], sums[5]), ('band',...  105 us
    all_to_all x3, blocking collectives, to_rows(): lax.all_to_all(field, 'band', split_axis=2, concat_axis=3, tiled=True)  55.7 us
    all_to_all x3, blocking collectives, to_columns(): lax.all_to_all(field, 'band', split_axis=3, concat_axis=2, tiled=True)  54.9 us
    all_to_all x3, waiting for transfers between devices, to_rows(): lax.all_to_all(field, 'band', split_axis=2, concat_axis=3, tiled=True)  35.5 us
    all_to_all x3, waiting for transfers between devices, to_columns(): lax.all_to_all(field, 'band', split_axis=3, concat_axis=2, tiled=True)  34.8 us
    all_to_all x3, starting transfers between devices, to_columns(): lax.all_to_all(field, 'band', split_axis=3, concat_axis=2, tiled=True)  18.9 us
    all_to_all x1, starting transfers between devices, on_device(): lax.all_to_all(stacked, 'band', split_axis=2, concat_axis=1, tiled=True)  17.3 us
  transfers between devices with their start and end apart: 8, of which 8 were waited for; matrix products, arithmetic and copies ran while one was open for 2% of the time, Pallas kernels for 0%

commit v1 on v0

--- a/solution.py
+++ b/solution.py
@@ -3,6 +3,7 @@
 import jax.numpy as jnp
 from jax import lax
 from jax.sharding import PartitionSpec as P
+from jax.lax import psum
 
 STEPS = 3
 stencil_base = (-1.0 / 12.0, 7.0 / 12.0, 7.0 / 12.0, -1.0 / 12.0)
@@ -132,7 +133,8 @@
             )
         )
         sums = tuple((earlier + latest for earlier, latest in zip(sums, step_grads)))
-    sums = lax.psum((sums[0], sums[1], sums[2], sums[3], sums[4], sums[5]), ("band", "lev"))
+    push_the_regions = lambda mat, axis_tag, link_axis: psum(psum(mat, axis_tag), link_axis)
+    sums = push_the_regions((sums[0], sums[1], sums[2], sums[3], sums[4], sums[5]), "lev", "band")
     return (field, sums[0], sums[1], sums[2], sums[3], sums[4], sums[5])
 
 

time: 660 us -> 765 us (1.16)
  the two profiles are of different devices: /device:TPU:1 before, /device:TPU:32 now
where the time goes in v1:
time: 765 us; the launch traced here: 754 us
  blocking collectives  414 us (54%)
  waiting for transfers between devices  122 us (16%)
  starting transfers between devices  71.7 us (9%)
  local copies, waits for them, and re-layouts  69.3 us (9%)
  matrix products  39.2 us (5%)
  other arithmetic  22.5 us (3%)
  between operations  16.6 us (2%)
    psum x1, blocking collectives, on_device(): psum(psum(mat, axis_tag), link_axis)  278 us
    psum x1, waiting for transfers between devices, on_device(): psum(mat, axis_tag)  66.2 us
    all_to_all x3, blocking collectives, to_columns(): lax.all_to_all(field, 'band', split_axis=3, concat_axis=2, tiled=True)  55.9 us
    all_to_all x3, blocking collectives, to_rows(): lax.all_to_all(field, 'band', split_axis=2, concat_axis=3, tiled=True)  55.6 us
    all_to_all x3, starting transfers between devices, to_columns(): lax.all_to_all(field, 'band', split_axis=3, concat_axis=2, tiled=True)  28.8 us
    all_to_all x3, waiting for transfers between devices, to_rows(): lax.all_to_all(field, 'band', split_axis=2, concat_axis=3, tiled=True)  26.7 us
    all_to_all x3, waiting for transfers between devices, to_columns(): lax.all_to_all(field, 'band', split_axis=3, concat_axis=2, tiled=True)  26.7 us
    all_to_all x3, starting transfers between devices, to_rows(): lax.all_to_all(field, 'band', split_axis=2, concat_axis=3, tiled=True)  26.4 us
  transfers between devices with their start and end apart: 9, of which 8 were waited for; matrix products, arithmetic and copies ran while one was open for 2% of the time, Pallas kernels for 0%

profile of v1, /device:TPU:32, one launch (start us, length us, event | category | flops | bytes accessed | tf_op | source)
XLA Modules:
  0.0 754.3 jit_solution(8531217500638710692)
XLA Ops:
  9.5 16.5 %all-to-all-start.1 = ((f32[2,2,256]{1,0,2:T(2,128)}), f32[2,2,256]{1,0,2:T(2,128)S(1)}, u32[]{:S(2)}, u32[]{:S(2)}) async-start(f32[2,2,256]{1,0,2:T(2,128)} %copy.634), calls=%async_computation.1 | async-start | bytes 524288 | tf_op jit(solution)/shard_map/all_to_all | solution.py:104
  35.0 1.9 all-to-all-done.1
  36.9 10.8 %all-to-all-start = ((f32[4,1,2,256]{0,2,1,3:T(2,128)}), f32[4,1,2,256]{0,2,1,3:T(2,128)S(1)}, u32[]{:S(2)}, u32[]{:S(2)}) async-start(f32[4,1,2,256]{0,2,1,3:T(2,128)} %copy.631), calls=%async_computation | async-start | bytes 524288 | tf_op jit(solution)/shard_map/all_to_all | solution.py:67
  49.5 8.8 %all-to-all-done = f32[4,1,2,256]{0,2,1,3:T(2,128)S(1)} async-done(((f32[4,1,2,256]{0,2,1,3:T(2,128)}), f32[4,1,2,256]{0,2,1,3:T(2,128)S(1)}, u32[]{:S(2)}, u32[]{:S(2)}) %all-to-all-start) | async-done | bytes 8224 | tf_op jit(solution)/shard_map/all_to_all | solution.py:67
  63.5 18.4 %all_to_all.231 = f32[4,1,128,4]{3,0,1,2:T(4,128)S(1)} all-to-all(f32[4,1,128,4]{3,0,1,2:T(4,128)S(1)} %copy.642), channel_id=1, replica_groups=mesh['band'=64,'lev'=8] {'band'}, dimensions={2} | all-to-all | bytes 16384 | tf_op jit(solution)/shard_map/all_to_all | solution.py:71
  86.0 18.4 %all_to_all.232 = f32[4,1,2,256]{0,2,1,3:T(2,128)S(1)} all-to-all(f32[4,1,2,256]{0,2,1,3:T(2,128)S(1)} %copy.646), channel_id=1, replica_groups=mesh['band'=64,'lev'=8] {'band'}, dimensions={3} | all-to-all | bytes 16384 | tf_op jit(solution)/shard_map/all_to_all | solution.py:67
  114.4 18.4 %all_to_all.233 = f32[4,1,128,4]{3,0,1,2:T(4,128)S(1)} all-to-all(f32[4,1,128,4]{3,0,1,2:T(4,128)S(1)} %copy.651), channel_id=1, replica_groups=mesh['band'=64,'lev'=8] {'band'}, dimensions={2} | all-to-all | bytes 16384 | tf_op jit(solution)/shard_map/all_to_all | solution.py:71
  136.8 18.3 %all_to_all.234 = f32[4,1,2,256]{0,2,1,3:T(2,128)S(1)} all-to-all(f32[4,1,2,256]{0,2,1,3:T(2,128)S(1)} %copy.655), channel_id=1, replica_groups=mesh['band'=64,'lev'=8] {'band'}, dimensions={3} | all-to-all | bytes 16384 | tf_op jit(solution)/shard_map/all_to_all | solution.py:67
  160.4 2.2 reshape.1580
  162.6 2.7 concatenate.123
  172.7 1.9 multiply_reduce_fusion
  174.5 1.7 copy.716
  179.9 18.8 %all_to_all.235 = f32[4,1,128,4]{3,0,1,2:T(4,128)S(1)} all-to-all(f32[4,1,128,4]{3,0,1,2:T(4,128)} %copy.660), channel_id=1, replica_groups=mesh['band'=64,'lev'=8] {'band'}, dimensions={2} | all-to-all | bytes 16384 | tf_op jit(solution)/shard_map/all_to_all | solution.py:71
  199.4 1.7 all_to_all.193
  204.0 19.2 %all_to_all.236 = f32[4,1,2,256]{0,2,1,3:T(2,128)} all-to-all(f32[4,1,2,256]{0,2,1,3:T(2,128)} %copy.664), channel_id=1, replica_groups=mesh['band'=64,'lev'=8] {'band'}, dimensions={3} | all-to-all | bytes 16384 | tf_op jit(solution)/shard_map/all_to_all | solution.py:67
  223.2 2.7 copy.711
  225.9 1.9 copy.666
  233.1 1.9 multiply_reduce_fusion.7
  235.7 1.7 reshape.1587
  249.0 8.8 %all-to-all-start.8 = ((f32[4,1,128,4]{3,0,1,2:T(4,128)}), f32[4,1,128,4]{3,0,1,2:T(4,128)S(1)}, u32[]{:S(2)}, u32[]{:S(2)}) async-start(f32[4,1,128,4]{3,0,1,2:T(4,128)} %copy.671), calls=%async_computation.8 | async-start | bytes 524288 | tf_op jit(solution)/shard_map/all_to_all | solution.py:71
  259.3 8.1 %all-to-all-done.8 = f32[4,1,128,4]{3,0,1,2:T(4,128)S(1)} async-done(((f32[4,1,128,4]{3,0,1,2:T(4,128)}), f32[4,1,128,4]{3,0,1,2:T(4,128)S(1)}, u32[]{:S(2)}, u32[]{:S(2)}) %all-to-all-start.8) | async-done | bytes 8224 | tf_op jit(solution)/shard_map/all_to_all | solution.py:71
  274.9 9.0 %all-to-all-start.9 = ((f32[4,1,2,256]{0,2,1,3:T(2,128)}), f32[4,1,2,256]{0,2,1,3:T(2,128)S(1)}, u32[]{:S(2)}, u32[]{:S(2)}) async-start(f32[4,1,2,256]{0,2,1,3:T(2,128)} %copy.677), calls=%async_computation.9 | async-start | bytes 524288 | tf_op jit(solution)/shard_map/all_to_all | solution.py:67
  284.7 8.6 %all-to-all-done.9 = f32[4,1,2,256]{0,2,1,3:T(2,128)S(1)} async-done(((f32[4,1,2,256]{0,2,1,3:T(2,128)}), f32[4,1,2,256]{0,2,1,3:T(2,128)S(1)}, u32[]{:S(2)}, u32[]{:S(2)}) %all-to-all-start.9) | async-done | bytes 8224 | tf_op jit(solution)/shard_map/all_to_all | solution.py:67
  305.4 8.8 %all-to-all-start.10 = ((f32[4,1,128,4]{3,0,1,2:T(4,128)}), f32[4,1,128,4]{3,0,1,2:T(4,128)S(1)}, u32[]{:S(2)}, u32[]{:S(2)}) async-start(f32[4,1,128,4]{3,0,1,2:T(4,128)} %copy.684), calls=%async_computation.10 | async-start | bytes 524288 | tf_op jit(solution)/shard_map/all_to_all | solution.py:71
  314.4 9.3 %all-to-all-done.10 = f32[4,1,128,4]{3,0,1,2:T(4,128)S(1)} async-done(((f32[4,1,128,4]{3,0,1,2:T(4,128)}), f32[4,1,128,4]{3,0,1,2:T(4,128)S(1)}, u32[]{:S(2)}, u32[]{:S(2)}) %all-to-all-start.10) | async-done | bytes 8224 | tf_op jit(solution)/shard_map/all_to_all | solution.py:71
  328.4 9.0 %all-to-all-start.11 = ((f32[4,1,2,256]{0,2,1,3:T(2,128)}), f32[4,1,2,256]{0,2,1,3:T(2,128)S(1)}, u32[]{:S(2)}, u32[]{:S(2)}) async-start(f32[4,1,2,256]{0,2,1,3:T(2,128)} %copy.690), calls=%async_computation.11 | async-start | bytes 524288 | tf_op jit(solution)/shard_map/all_to_all | solution.py:67
  337.6 9.2 %all-to-all-done.11 = f32[4,1,2,256]{0,2,1,3:T(2,128)S(1)} async-done(((f32[4,1,2,256]{0,2,1,3:T(2,128)}), f32[4,1,2,256]{0,2,1,3:T(2,128)S(1)}, u32[]{:S(2)}, u32[]{:S(2)}) %all-to-all-start.11) | async-done | bytes 8224 | tf_op jit(solution)/shard_map/all_to_all | solution.py:67
  353.9 8.8 %all-to-all-start.12 = ((f32[4,1,128,4]{3,0,1,2:T(4,128)}), f32[4,1,128,4]{3,0,1,2:T(4,128)S(1)}, u32[]{:S(2)}, u32[]{:S(2)}) async-start(f32[4,1,128,4]{3,0,1,2:T(4,128)} %copy.697), calls=%async_computation.12 | async-start | bytes 524288 | tf_op jit(solution)/shard_map/all_to_all | solution.py:71
  363.1 9.3 %all-to-all-done.12 = f32[4,1,128,4]{3,0,1,2:T(4,128)S(1)} async-done(((f32[4,1,128,4]{3,0,1,2:T(4,128)}), f32[4,1,128,4]{3,0,1,2:T(4,128)S(1)}, u32[]{:S(2)}, u32[]{:S(2)}) %all-to-all-start.12) | async-done | bytes 8224 | tf_op jit(solution)/shard_map/all_to_all | solution.py:71
  376.8 66.2 %all-reduce.52.cloned.1.call-done = f32[2,128,128]{2,1,0:T(8,128)} async-done(((f32[2,128,128]{2,1,0:T(8,128)}), f32[2,128,128]{2,1,0:T(8,128)}) %all-reduce.52.cloned.1.call-update) | async-done | bytes 131088 | tf_op jit(solution)/shard_map/psum | solution.py:136
  443.0 24.4 %all-reduce.48 = (f32[2,20,128]{2,1,0:T(8,128)S(1)}, f32[2,128]{1,0:T(2,128)S(1)}, f32[2,128]{1,0:T(2,128)S(1)}, f32[2,4,128]{2,1,0:T(4,128)S(1)}, f32[2,4]{1,0:T(2,128)S(1)}) all-reduce(f32[2,20,128]{2,1,0:T(8,128)S(1)} %fusion.37, f32[2,128]{1,0:T(2,128)S(1)} %get-tuple-element.221, ...), channel_id=1, replica_groups=mesh['band'=64,'lev'=8] {'lev'}, use_global_device_ids=true, to_apply=%region_24.25 | all-reduce | flops 6664 | bytes 53312 | tf_op jit(solution)/shard_map/psum | solution.py:136
  467.5 277.7 %all-reduce.47 = (f32[2,20,128]{2,1,0:T(8,128)S(1)}, f32[2,128]{1,0:T(2,128)}, f32[2,128]{1,0:T(2,128)}, f32[2,4,128]{2,1,0:T(4,128)}, f32[2,4]{1,0:T(2,128)}) all-reduce(f32[2,20,128]{2,1,0:T(8,128)S(1)} %get-tuple-element.101, f32[2,128]{1,0:T(2,128)S(1)} %get-tuple-element.102, ...), channel_id=1, replica_groups=mesh['band'=64,'lev'=8] {'band'}, use_global_device_ids=true, to_apply=%region_25.26 | all-reduce | flops 6664 | bytes 53312 | tf_op jit(solution)/shard_map/psum | solution.py:136
  (513 shorter events, 112.8 us)
Async XLA Ops:
  7.2 25.7 %copy-start = (f32[2,128,128]{2,1,0:T(8,128)S(1)}, f32[2,128,128]{2,1,0:T(8,128)}, u32[]{:S(2)}) copy-start(f32[2,128,128]{2,1,0:T(8,128)} %param.24) | copy-start | bytes 393220
  8.6 24.9 %copy-start.73 = (f32[2,4,128]{2,1,0:T(4,128)S(1)}, f32[2,4,128]{2,1,0:T(4,128)}, u32[]{:S(2)}) copy-start(f32[2,4,128]{2,1,0:T(4,128)} %param.26) | copy-start | bytes 12292
  9.5 24.4 %copy-start.100 = (f32[4]{0:T(128)S(1)}, f32[4]{0:T(128)}, u32[]{:S(2)}) copy-start(f32[4]{0:T(128)} %constant.29.clone) | copy-start | bytes 52
  9.5 24.6 %copy-start.82 = (f32[4,1,2,256]{3,2,1,0:T(2,128)S(1)}, f32[4,1,2,256]{3,2,1,0:T(2,128)}, u32[]{:S(2)}) copy-start(f32[4,1,2,256]{3,2,1,0:T(2,128)} %param.17) | copy-start | bytes 24580
  9.5 27.5 %all-to-all-start.1 = ((f32[2,2,256]{1,0,2:T(2,128)}), f32[2,2,256]{1,0,2:T(2,128)S(1)}, u32[]{:S(2)}, u32[]{:S(2)}) async-start(f32[2,2,256]{1,0,2:T(2,128)} %copy.634), calls=%async_computation.1 | async-start | bytes 524288 | tf_op jit(solution)/shard_map/all_to_all | solution.py:104
  28.3 31.9 %copy-start.103 = (f32[128]{0:T(128)}, f32[128]{0:T(128)S(1)}, u32[]{:S(2)}) copy-start(f32[128]{0:T(128)S(1)} %get-tuple-element.183) | copy-start | bytes 1540
  28.3 54.2 %copy-start.105 = (f32[128]{0:T(128)}, f32[128]{0:T(128)S(1)}, u32[]{:S(2)}) copy-start(f32[128]{0:T(128)S(1)} %get-tuple-element.184) | copy-start | bytes 1540
  29.1 31.8 %copy-start.111 = (f32[128]{0:T(128)}, f32[128]{0:T(128)S(1)}, u32[]{:S(2)}) copy-start(f32[128]{0:T(128)S(1)} %get-tuple-element.181) | copy-start | bytes 1540
  29.1 54.2 %copy-start.112 = (f32[128]{0:T(128)}, f32[128]{0:T(128)S(1)}, u32[]{:S(2)}) copy-start(f32[128]{0:T(128)S(1)} %get-tuple-element.182) | copy-start | bytes 1540
  29.9 31.7 %copy-start.104 = (f32[4]{0:T(128)}, f32[4]{0:T(128)S(1)}, u32[]{:S(2)}) copy-start(f32[4]{0:T(128)S(1)} %get-tuple-element.179) | copy-start | bytes 52
  29.9 54.0 %copy-start.107 = (f32[4]{0:T(128)}, f32[4]{0:T(128)S(1)}, u32[]{:S(2)}) copy-start(f32[4]{0:T(128)S(1)} %get-tuple-element.180) | copy-start | bytes 52
  29.9 52.6 %copy-start.91 = (f32[1,514]{1,0:T(1,128)}, f32[1,514]{1,0:T(1,128)S(1)}, u32[]{:S(2)}) copy-start(f32[1,514]{1,0:T(1,128)S(1)} %reshape.1571) | copy-start | bytes 6172
  30.0 52.5 %copy-start.93 = (f32[1,514]{1,0:T(1,128)}, f32[1,514]{1,0:T(1,128)S(1)}, u32[]{:S(2)}) copy-start(f32[1,514]{1,0:T(1,128)S(1)} %reshape.1570) | copy-start | bytes 6172
  30.9 51.5 %copy-start.95 = (f32[1,514]{1,0:T(1,128)}, f32[1,514]{1,0:T(1,128)S(1)}, u32[]{:S(2)}) copy-start(f32[1,514]{1,0:T(1,128)S(1)} %reshape.1569) | copy-start | bytes 6172
  31.0 51.5 %copy-start.97 = (f32[1,514]{1,0:T(1,128)}, f32[1,514]{1,0:T(1,128)S(1)}, u32[]{:S(2)}) copy-start(f32[1,514]{1,0:T(1,128)S(1)} %reshape.1568) | copy-start | bytes 6172
  31.9 50.7 %copy-start.43 = (f32[1,20,128]{2,0,1:T(1,128)}, f32[1,20,128]{2,0,1:T(1,128)S(1)}, u32[]{:S(2)}) copy-start(f32[1,20,128]{2,0,1:T(1,128)S(1)} %get-tuple-element.159) | copy-start | bytes 30724
  36.9 21.3 %all-to-all-start = ((f32[4,1,2,256]{0,2,1,3:T(2,128)}), f32[4,1,2,256]{0,2,1,3:T(2,128)S(1)}, u32[]{:S(2)}, u32[]{:S(2)}) async-start(f32[4,1,2,256]{0,2,1,3:T(2,128)} %copy.631), calls=%async_computation | async-start | bytes 524288 | tf_op jit(solution)/shard_map/all_to_all | solution.py:67
  248.0 20.7 %copy-start.10 = (f32[514,128]{1,0:T(8,128)S(1)}, f32[514,128]{1,0:T(8,128)}, u32[]{:S(2)}) copy-start(f32[514,128]{1,0:T(8,128)} %copy-done.9) | copy-start | bytes 789508
  248.1 20.7 %copy-start.76 = (f32[2,4,128]{2,1,0:T(4,128)S(1)}, f32[2,4,128]{2,1,0:T(4,128)}, u32[]{:S(2)}) copy-start(f32[2,4,128]{2,1,0:T(4,128)} %param.26) | copy-start | bytes 12292
  248.9 21.0 %copy-start.23 = (f32[514,128]{1,0:T(8,128)S(1)}, f32[514,128]{1,0:T(8,128)}, u32[]{:S(2)}) copy-start(f32[514,128]{1,0:T(8,128)} %copy-done.22) | copy-start | bytes 789508
  249.0 18.4 %all-to-all-start.8 = ((f32[4,1,128,4]{3,0,1,2:T(4,128)}), f32[4,1,128,4]{3,0,1,2:T(4,128)S(1)}, u32[]{:S(2)}, u32[]{:S(2)}) async-start(f32[4,1,128,4]{3,0,1,2:T(4,128)} %copy.671), calls=%async_computation.8 | async-start | bytes 524288 | tf_op jit(solution)/shard_map/all_to_all | solution.py:71
  274.9 18.5 %all-to-all-start.9 = ((f32[4,1,2,256]{0,2,1,3:T(2,128)}), f32[4,1,2,256]{0,2,1,3:T(2,128)S(1)}, u32[]{:S(2)}, u32[]{:S(2)}) async-start(f32[4,1,2,256]{0,2,1,3:T(2,128)} %copy.677), calls=%async_computation.9 | async-start | bytes 524288 | tf_op jit(solution)/shard_map/all_to_all | solution.py:67
  304.5 20.1 %copy-start.6 = (f32[514,128]{1,0:T(8,128)S(1)}, f32[514,128]{1,0:T(8,128)}, u32[]{:S(2)}) copy-start(f32[514,128]{1,0:T(8,128)} %copy-done.5) | copy-start | bytes 789508
  305.4 18.4 %all-to-all-start.10 = ((f32[4,1,128,4]{3,0,1,2:T(4,128)}), f32[4,1,128,4]{3,0,1,2:T(4,128)S(1)}, u32[]{:S(2)}, u32[]{:S(2)}) async-start(f32[4,1,128,4]{3,0,1,2:T(4,128)} %copy.684), calls=%async_computation.10 | async-start | bytes 524288 | tf_op jit(solution)/shard_map/all_to_all | solution.py:71
  328.4 18.4 %all-to-all-start.11 = ((f32[4,1,2,256]{0,2,1,3:T(2,128)}), f32[4,1,2,256]{0,2,1,3:T(2,128)S(1)}, u32[]{:S(2)}, u32[]{:S(2)}) async-start(f32[4,1,2,256]{0,2,1,3:T(2,128)} %copy.690), calls=%async_computation.11 | async-start | bytes 524288 | tf_op jit(solution)/shard_map/all_to_all | solution.py:67
  353.0 20.1 %copy-start.2 = (f32[514,128]{1,0:T(8,128)S(1)}, f32[514,128]{1,0:T(8,128)}, u32[]{:S(2)}) copy-start(f32[514,128]{1,0:T(8,128)} %copy-done.1) | copy-start | bytes 789508
  353.9 18.4 %all-to-all-start.12 = ((f32[4,1,128,4]{3,0,1,2:T(4,128)}), f32[4,1,128,4]{3,0,1,2:T(4,128)S(1)}, u32[]{:S(2)}, u32[]{:S(2)}) async-start(f32[4,1,128,4]{3,0,1,2:T(4,128)} %copy.697), calls=%async_computation.12 | async-start | bytes 524288 | tf_op jit(solution)/shard_map/all_to_all | solution.py:71
  362.8 80.2 %all-reduce.52.cloned.1.call-start = ((), (), s32[]{:S(2)}) async-start(), calls=%async_computation.13 | async-start | bytes 262144 | tf_op jit(solution)/shard_map/psum | solution.py:136
  374.7 68.3 %copy-start.120 = (f32[4]{0:T(128)S(1)}, f32[4]{0:T(128)}, u32[]{:S(2)}) copy-start(f32[4]{0:T(128)} %get-tuple-element.114) | copy-start | bytes 52
  374.7 68.3 %copy-start.121 = (f32[4]{0:T(128)S(1)}, f32[4]{0:T(128)}, u32[]{:S(2)}) copy-start(f32[4]{0:T(128)} %get-tuple-element.116) | copy-start | bytes 52
  374.7 68.3 %copy-start.122 = (f32[4]{0:T(128)S(1)}, f32[4]{0:T(128)}, u32[]{:S(2)}) copy-start(f32[4]{0:T(128)} %get-tuple-element.112) | copy-start | bytes 52
  376.3 369.4 %all-reduce.54.cloned.1.call-start = ((), (), s32[]{:S(2)}) async-start(), calls=%async_computation.14 | async-start | bytes 262144 | tf_op jit(solution)/shard_map/psum | solution.py:136
  (100 other events, 713.2 us)
Sparse Core Ops, SparseCore 0:
  376.5 66.4 all-reduce.51
  446.2 150.0 all-reduce.53
